TPU v7x, 512 devices: a whole 4x4x16 slice. The times are simulated.
512 devices in a mesh: batch: 8 (over x, core), head: 2 (over z_hi), expert: 32 (over z_lo, y).
Axes of the slice: x: 4, y: 4, z: 16 (z_hi: 2, z_lo: 8; z = z_hi * 8 + z_lo), core: 2. Of those that a mesh axis runs over, the one named last changes fastest.
Arguments:
- hidden_in: bfloat16 [65536, 2048], P(('batch', 'head', 'expert')), may hold values from -6 to 6
- norm_gain: float32 [2048], replicated, may hold values from 0.25 to 1.75
- w_gate: bfloat16 [64, 2048, 384], P('expert', ('batch', 'head')), may hold values from -0.125 to 0.125
- w_up: bfloat16 [64, 2048, 384], P('expert', ('batch', 'head')), may hold values from -0.125 to 0.125
- w_down: bfloat16 [64, 384, 2048], P('expert', None, ('batch', 'head')), may hold values from -0.3125 to 0.3125
- expert_ids: int32 [65536, 2], P(('batch', 'head', 'expert')), may hold values from 0 to 63, all different within a row; in each aligned block of 128 rows (0 to 127, 128 to 255, ...) at most 6 rows name the same one
- gate_codes: int32 [65536, 2], P(('batch', 'head', 'expert')), may hold values from 4096 to 65535
- out_grad: bfloat16 [65536, 2048], P(('batch', 'head', 'expert')), may hold values from -6 to 6
Outputs:
- output: bfloat16 [65536, 2048], P(('batch', 'head', 'expert'))
- grad_in: bfloat16 [65536, 2048], P(('batch', 'head', 'expert'))
Inputs may be any that keep to these rules, and one draw needn't show every extreme that they name: `expert_ids`: each row names 2 different experts; within the rows of one device no expert is named more than 6 times, a bound that some block reaches.
All inputs are finite; a program needn't handle non-finite values.
Results may differ from a plain program's by a relative error of at most 0.0055.
Values may be sent and summed in bfloat16 or wider, within the bound.
No kernel may reach another device: no remote copies, remote signals or barrier semaphores. Data moves between devices by JAX's collectives and lax.ppermute only.
A program may use at most 128 MiB of HBM per device.

v0:
```python
import jax
import jax.numpy as jnp
from jax import lax
from jax.sharding import PartitionSpec as P

epsilon = 1e-06


def in_order(tiles, dim):
    tiles = jnp.moveaxis(tiles, 0, dim)
    shape = tiles.shape
    return tiles.reshape(*shape[:dim], shape[dim] * shape[dim + 1], *shape[dim + 2 :])


def copy_for_each(value, axis):
    length = lax.axis_size(axis)
    return lax.all_to_all(
        jnp.broadcast_to(value[None], (length, *value.shape)), axis, 0, 0, tiled=True
    )


def collect(value, axis, dim):
    return in_order(copy_for_each(value, axis), dim)


def side_by_side(arrays, axis, dim, along):
    ends, at = ([], 0)
    for a in arrays[:-1]:
        at += a.shape[along]
        ends.append(at)
    both = jnp.concatenate(arrays, axis=along)
    return tuple(jnp.split(collect(both, axis, dim), ends, axis=along))


def gather_turned(arrays, axis, dims):
    turned = [jnp.moveaxis(a, dim, 0) for a, dim in zip(arrays, dims)]
    both = jnp.concatenate([t.reshape(len(t), -1) for t in turned], axis=1)
    filled, at, finished = (lax.all_gather(both, axis, axis=0, tiled=True), 0, [])
    for t, dim in zip(turned, dims):
        section = filled[:, at : at + t[0].size].reshape(-1, *t.shape[1:])
        finished.append(jnp.moveaxis(section, 0, dim))
        at += t[0].size
    return tuple(finished)


def slot_tables(expert_ids, expert_total, capacity):
    chosen = expert_ids.shape[1]
    routes = expert_ids.reshape(-1)
    route_total = routes.shape[0]
    labels = jnp.arange(expert_total, dtype=jnp.int32)
    onehot = (routes[:, None] == labels[None, :]).astype(jnp.int32)
    before = jnp.cumsum(onehot, axis=0) - onehot
    position = jnp.sum(before * onehot, axis=1)
    slot_ids = routes * capacity + position
    owner_rows = jnp.arange(route_total, dtype=jnp.int32) // chosen
    source_rows = jnp.zeros((expert_total * capacity,), jnp.int32).at[slot_ids].set(owner_rows)
    filled = jnp.zeros((expert_total * capacity,), jnp.int32).at[slot_ids].set(1)
    return (slot_ids, source_rows, filled)


def expert_forward(slot_rows, gate_mat, up_mat, down_mat):
    gate_pre = jnp.dot(slot_rows, gate_mat, preferred_element_type=jnp.float32)
    up_pre = jnp.dot(slot_rows, up_mat, preferred_element_type=jnp.float32)
    inner_rows = (jax.nn.silu(gate_pre) * up_pre).astype(jnp.bfloat16)
    result = jnp.dot(inner_rows, down_mat, preferred_element_type=jnp.float32).astype(jnp.bfloat16)
    return (result, gate_pre, up_pre)


def expert_backward(slot_grads, gate_pre, up_pre, gate_mat, up_mat, down_mat):
    back_grad = jnp.dot(slot_grads, down_mat.T, preferred_element_type=jnp.float32)
    sigmoid_gate = jax.nn.sigmoid(gate_pre)
    grad_gate = (
        back_grad * up_pre * sigmoid_gate * (1.0 + gate_pre * (1.0 - sigmoid_gate))
    ).astype(jnp.bfloat16)
    grad_up = (back_grad * jax.nn.silu(gate_pre)).astype(jnp.bfloat16)
    grad_rows = jnp.dot(grad_gate, gate_mat.T, preferred_element_type=jnp.float32)
    grad_rows = grad_rows + jnp.dot(grad_up, up_mat.T, preferred_element_type=jnp.float32)
    return grad_rows.astype(jnp.bfloat16)


def body(hidden_in, norm_gain, w_gate, w_up, w_down, expert_ids, gate_codes, out_grad):
    owners = lax.axis_size("expert")
    local_count = w_gate.shape[0]
    expert_total = owners * local_count
    tok_rows, features = hidden_in.shape
    chosen = expert_ids.shape[1]
    capacity = 3 * tok_rows * chosen // (2 * expert_total)
    hidden_float = hidden_in.astype(jnp.float32)
    row_scale = lax.rsqrt(jnp.mean(hidden_float * hidden_float, axis=1, keepdims=True) + epsilon)
    normed = (hidden_float * row_scale * norm_gain).astype(jnp.bfloat16)
    code_values = gate_codes.astype(jnp.float32)
    weights = code_values / jnp.sum(code_values, axis=1, keepdims=True)
    slot_ids, source_rows, filled = slot_tables(expert_ids, expert_total, capacity)
    order_rows = source_rows.reshape(owners, local_count, capacity).transpose(1, 0, 2).reshape(-1)
    order_live = filled.reshape(owners, local_count, capacity).transpose(1, 0, 2).reshape(-1)
    keep = (order_live == 1)[:, None]
    nothing = jnp.zeros((), jnp.bfloat16)
    slot_shape = (local_count, owners, capacity, features)
    flat_shape = (local_count, owners * capacity, features)
    send_normed = jnp.where(keep, normed[order_rows], nothing).reshape(slot_shape)
    send_grad = jnp.where(keep, out_grad[order_rows], nothing).reshape(slot_shape)
    gate_pair, up_pair, down_pair = (
        *side_by_side((w_gate, w_up), "head", 1, 0),
        collect(w_down, "head", 2),
    )
    gate_full, up_full, down_full = gather_turned(
        (gate_pair, up_pair, down_pair), "batch", (1, 1, 2)
    )
    forward = jax.vmap(expert_forward)
    backward = jax.vmap(expert_backward)
    arrived, arrived_grad = (
        lax.all_to_all(send_normed, "expert", split_axis=1, concat_axis=1, tiled=True),
        lax.all_to_all(send_grad, "expert", split_axis=1, concat_axis=1, tiled=True),
    )
    result, gate_pre, up_pre = forward(arrived.reshape(flat_shape), gate_full, up_full, down_full)
    grad_rows = backward(
        arrived_grad.reshape(flat_shape), gate_pre, up_pre, gate_full, up_full, down_full
    )
    returned, returned_grad = (
        lax.all_to_all(
            result.reshape(slot_shape), "expert", split_axis=1, concat_axis=1, tiled=True
        ),
        lax.all_to_all(
            grad_rows.reshape(slot_shape), "expert", split_axis=1, concat_axis=1, tiled=True
        ),
    )
    expert_of = slot_ids // capacity
    position = slot_ids % capacity
    flat_index = (expert_of % local_count * owners + expert_of // local_count) * capacity + position
    picked = (
        returned.reshape(-1, features)[flat_index]
        .astype(jnp.float32)
        .reshape(tok_rows, chosen, features)
    )
    mixture = jnp.sum(picked * weights[:, :, None], axis=1)
    output = (hidden_float + mixture).astype(jnp.bfloat16)
    picked_grad = (
        returned_grad.reshape(-1, features)[flat_index]
        .astype(jnp.float32)
        .reshape(tok_rows, chosen, features)
    )
    grad_normed = jnp.sum(picked_grad * weights[:, :, None], axis=1)
    scaled = norm_gain * grad_normed
    inner_mean = jnp.mean(scaled * hidden_float, axis=1, keepdims=True)
    grad_in = (
        out_grad.astype(jnp.float32)
        + row_scale * scaled
        - hidden_float * (row_scale * row_scale * row_scale) * inner_mean
    )
    return (output, grad_in.astype(jnp.bfloat16))


def solution(mesh):
    in_specs = (
        P(("batch", "head", "expert"), None),
        P(),
        P("expert", ("batch", "head"), None),
        P("expert", ("batch", "head"), None),
        P("expert", None, ("batch", "head")),
        P(("batch", "head", "expert"), None),
        P(("batch", "head", "expert"), None),
        P(("batch", "head", "expert"), None),
    )
    out_specs = (P(("batch", "head", "expert"), None), P(("batch", "head", "expert"), None))
    return jax.shard_map(body, mesh=mesh, in_specs=in_specs, out_specs=out_specs, check_vma=False)
```

profile of v0, /device:TPU:1, one launch (start us, length us, event | category | flops | bytes accessed | tf_op | source)
XLA Modules:
  0.0 477.5 jit_solution(2065011808514558171)
XLA Ops:
  8.9 15.6 %all-to-all-start.2 = ((bf16[2,2,384,128]{3,2,1,0:T(8,128)(2,1)}), bf16[2,2,384,128]{3,2,1,0:T(8,128)(2,1)S(1)}, u32[]{:S(2)}, u32[]{:S(2)}) async-start(bf16[2,2,384,128]{3,2,1,0:T(8,128)(2,1)} %broadcast_in_dim.26), calls=%async_computation.2 | async-start | bytes 786432 | tf_op jit(solution)/shard_map/all_to_all | solution.py:17
  25.8 13.2 %all-to-all-done.2 = bf16[2,2,384,128]{3,2,1,0:T(8,128)(2,1)S(1)} async-done(((bf16[2,2,384,128]{3,2,1,0:T(8,128)(2,1)}), bf16[2,2,384,128]{3,2,1,0:T(8,128)(2,1)S(1)}, u32[]{:S(2)}, u32[]{:S(2)}) %all-to-all-start.2) | async-done | bytes 393248 | tf_op jit(solution)/shard_map/all_to_all | solution.py:17
  40.0 3.5 all-to-all-start.1
  44.0 17.1 %all-to-all-done.1 = bf16[2,4,128,384]{2,3,1,0:T(8,128)(2,1)S(1)} async-done(((bf16[2,4,128,384]{2,3,1,0:T(8,128)(2,1)}), bf16[2,4,128,384]{2,3,1,0:T(8,128)(2,1)S(1)}, u32[]{:S(2)}, u32[]{:S(2)}) %all-to-all-start.1) | async-done | bytes 786464 | tf_op jit(solution)/shard_map/all_to_all | solution.py:17
  66.5 3.1 gather_fusion.2
  75.2 3.1 gather_fusion
  78.4 3.7 gather.17
  82.1 3.3 broadcast_select_fusion
  88.2 39.4 %all-to-all-start = ((bf16[2,32,6,2048]{3,0,2,1:T(2,128)(2,1)}), bf16[2,32,6,2048]{3,0,2,1:T(2,128)(2,1)}, u32[]{:S(2)}, u32[]{:S(2)}) async-start(bf16[2,32,6,2048]{3,0,2,1:T(2,128)(2,1)} %copy.83), calls=%async_computation | async-start | bytes 3145728 | tf_op jit(solution)/shard_map/all_to_all | solution.py:112
  130.5 69.3 %all-to-all-done = bf16[2,32,6,2048]{3,0,2,1:T(2,128)(2,1)} async-done(((bf16[2,32,6,2048]{3,0,2,1:T(2,128)(2,1)}), bf16[2,32,6,2048]{3,0,2,1:T(2,128)(2,1)}, u32[]{:S(2)}, u32[]{:S(2)}) %all-to-all-start) | async-done | bytes 1572896 | tf_op jit(solution)/shard_map/all_to_all | solution.py:112
  199.8 7.9 %all-to-all-start.4 = ((bf16[2,32,6,2048]{3,0,2,1:T(2,128)(2,1)}), bf16[2,32,6,2048]{3,0,2,1:T(2,128)(2,1)S(1)}, u32[]{:S(2)}, u32[]{:S(2)}) async-start(bf16[2,32,6,2048]{3,0,2,1:T(2,128)(2,1)} %copy.97), calls=%async_computation.4 | async-start | bytes 3145728 | tf_op jit(solution)/shard_map/all_to_all | solution.py:113
  207.7 6.7 %fusion.36 = (bf16[2048,768]{0,1:T(8,128)(2,1)}, bf16[2048,768]{0,1:T(8,128)(2,1)}, bf16[2048,768]{0,1:T(8,128)(2,1)}) fusion(bf16[2048,2304]{0,1:T(8,128)(2,1)} %all-gather.2.cloned.1.call-done), kind=kLoop, calls=%fused_computation.85 | loop fusion | bytes 18874368 | tf_op jit(solution)/shard_map/slice | solution.py:40
  214.4 4.6 copy.90
  219.0 4.7 copy.92
  223.7 3.8 fusion.2
  230.4 49.3 %all-to-all-done.4 = bf16[2,32,6,2048]{3,0,2,1:T(2,128)(2,1)S(1)} async-done(((bf16[2,32,6,2048]{3,0,2,1:T(2,128)(2,1)}), bf16[2,32,6,2048]{3,0,2,1:T(2,128)(2,1)S(1)}, u32[]{:S(2)}, u32[]{:S(2)}) %all-to-all-start.4) | async-done | bytes 1572896 | tf_op jit(solution)/shard_map/all_to_all | solution.py:113
  279.7 3.4 fusion.4
  288.9 8.3 %all-to-all-start.5 = ((bf16[2,32,6,2048]{3,0,2,1:T(2,128)(2,1)}), bf16[2,32,6,2048]{3,0,2,1:T(2,128)(2,1)S(1)}, u32[]{:S(2)}, u32[]{:S(2)}) async-start(bf16[2,32,6,2048]{3,0,2,1:T(2,128)(2,1)} %bitcast.69), calls=%async_computation.5 | async-start | bytes 3145728 | tf_op jit(solution)/shard_map/all_to_all | solution.py:123
  302.9 66.2 %all-to-all-done.5 = bf16[2,32,6,2048]{3,0,2,1:T(2,128)(2,1)S(1)} async-done(((bf16[2,32,6,2048]{3,0,2,1:T(2,128)(2,1)}), bf16[2,32,6,2048]{3,0,2,1:T(2,128)(2,1)S(1)}, u32[]{:S(2)}, u32[]{:S(2)}) %all-to-all-start.5) | async-done | bytes 1572896 | tf_op jit(solution)/shard_map/all_to_all | solution.py:123
  369.1 8.2 %all-to-all-start.3 = ((bf16[2,32,6,2048]{3,0,2,1:T(2,128)(2,1)}), bf16[2,32,6,2048]{3,0,2,1:T(2,128)(2,1)}, u32[]{:S(2)}, u32[]{:S(2)}) async-start(bf16[2,32,6,2048]{3,0,2,1:T(2,128)(2,1)} %bitcast.68), calls=%async_computation.3 | async-start | bytes 3145728 | tf_op jit(solution)/shard_map/all_to_all | solution.py:120
  385.9 63.4 %all-to-all-done.3 = bf16[2,32,6,2048]{3,0,2,1:T(2,128)(2,1)} async-done(((bf16[2,32,6,2048]{3,0,2,1:T(2,128)(2,1)}), bf16[2,32,6,2048]{3,0,2,1:T(2,128)(2,1)}, u32[]{:S(2)}, u32[]{:S(2)}) %all-to-all-start.3) | async-done | bytes 1572896 | tf_op jit(solution)/shard_map/all_to_all | solution.py:120
  449.4 3.4 copy.95
  457.8 3.5 reshape.324
  461.3 7.8 %multiply_reduce_fusion = (f32[128,2048]{1,0:T(8,128)S(1)}, f32[128,2048]{1,0:T(8,128)S(1)}) fusion(f32[128,2,2048]{2,1,0:T(2,128)S(1)} %copy-done.4, f32[128,2]{1,0:T(8,128)S(1)} %copy.96, f32[128,2,2048]{2,1,0:T(2,128)} %reshape.324), kind=kLoop, calls=%fused_computation.12 | loop fusion | flops 1572864 | bytes 6292480 | tf_op jit(solution)/shard_map/reduce_sum | solution.py:142
  (86 shorter events, 50.4 us)
Async XLA Ops:
  8.9 30.1 %all-to-all-start.2 = ((bf16[2,2,384,128]{3,2,1,0:T(8,128)(2,1)}), bf16[2,2,384,128]{3,2,1,0:T(8,128)(2,1)S(1)}, u32[]{:S(2)}, u32[]{:S(2)}) async-start(bf16[2,2,384,128]{3,2,1,0:T(8,128)(2,1)} %broadcast_in_dim.26), calls=%async_computation.2 | async-start | bytes 786432 | tf_op jit(solution)/shard_map/all_to_all | solution.py:17
  40.0 21.1 %all-to-all-start.1 = ((bf16[2,4,128,384]{2,3,1,0:T(8,128)(2,1)}), bf16[2,4,128,384]{2,3,1,0:T(8,128)(2,1)S(1)}, u32[]{:S(2)}, u32[]{:S(2)}) async-start(bf16[2,4,128,384]{2,3,1,0:T(8,128)(2,1)} %broadcast_in_dim.25), calls=%async_computation.1 | async-start | bytes 1572864 | tf_op jit(solution)/shard_map/all_to_all | solution.py:17
  43.5 164.2 %all-gather.2.cloned.1.call-start = ((), (), s32[]{:S(2)}) async-start(), calls=%async_computation.6 | async-start | bytes 10616832 | tf_op jit(solution)/shard_map/all_gather | solution.py:38
  61.7 1.3 copy-start.9
  61.9 4.6 copy-start
  69.6 4.2 copy-start.5
  69.6 4.4 copy-start.8
  88.2 39.5 %copy-start.3 = (bf16[2,32,6,2048]{3,2,1,0:T(8,128)(2,1)S(1)}, bf16[2,32,6,2048]{3,2,1,0:T(8,128)(2,1)}, u32[]{:S(2)}) copy-start(bf16[2,32,6,2048]{3,2,1,0:T(8,128)(2,1)} %get-tuple-element.11) | copy-start | bytes 4718596
  88.2 111.6 %all-to-all-start = ((bf16[2,32,6,2048]{3,0,2,1:T(2,128)(2,1)}), bf16[2,32,6,2048]{3,0,2,1:T(2,128)(2,1)}, u32[]{:S(2)}, u32[]{:S(2)}) async-start(bf16[2,32,6,2048]{3,0,2,1:T(2,128)(2,1)} %copy.83), calls=%async_computation | async-start | bytes 3145728 | tf_op jit(solution)/shard_map/all_to_all | solution.py:112
  199.8 80.0 %all-to-all-start.4 = ((bf16[2,32,6,2048]{3,0,2,1:T(2,128)(2,1)}), bf16[2,32,6,2048]{3,0,2,1:T(2,128)(2,1)S(1)}, u32[]{:S(2)}, u32[]{:S(2)}) async-start(bf16[2,32,6,2048]{3,0,2,1:T(2,128)(2,1)} %copy.97), calls=%async_computation.4 | async-start | bytes 3145728 | tf_op jit(solution)/shard_map/all_to_all | solution.py:113
  223.7 3.8 copy-start.7
  279.7 3.4 copy-start.2
  283.2 1.9 copy-start.1
  288.9 80.2 %all-to-all-start.5 = ((bf16[2,32,6,2048]{3,0,2,1:T(2,128)(2,1)}), bf16[2,32,6,2048]{3,0,2,1:T(2,128)(2,1)S(1)}, u32[]{:S(2)}, u32[]{:S(2)}) async-start(bf16[2,32,6,2048]{3,0,2,1:T(2,128)(2,1)} %bitcast.69), calls=%async_computation.5 | async-start | bytes 3145728 | tf_op jit(solution)/shard_map/all_to_all | solution.py:123
  302.9 74.4 %copy-start.10 = (s32[128,2]{0,1:T(2,128)S(1)}, s32[128,2]{0,1:T(2,128)}, u32[]{:S(2)}) copy-start(s32[128,2]{0,1:T(2,128)} %param.14) | copy-start | bytes 3076
  369.1 80.3 %all-to-all-start.3 = ((bf16[2,32,6,2048]{3,0,2,1:T(2,128)(2,1)}), bf16[2,32,6,2048]{3,0,2,1:T(2,128)(2,1)}, u32[]{:S(2)}, u32[]{:S(2)}) async-start(bf16[2,32,6,2048]{3,0,2,1:T(2,128)(2,1)} %bitcast.68), calls=%async_computation.3 | async-start | bytes 3145728 | tf_op jit(solution)/shard_map/all_to_all | solution.py:120
  457.8 3.5 copy-start.4
  461.3 7.8 %copy-start.6 = (bf16[128,2048]{1,0:T(8,128)(2,1)S(1)}, bf16[128,2048]{1,0:T(8,128)(2,1)}, u32[]{:S(2)}) copy-start(bf16[128,2048]{1,0:T(8,128)(2,1)} %param.8) | copy-start | bytes 1572868
Sparse Core Ops, SparseCore 0:
  63.2 91.7 all-gather.1
where the time goes:
time: 480 us; the launch traced here: 478 us
  waiting for transfers between devices  279 us (58%)
  starting transfers between devices  83.1 us (17%)
  local copies, waits for them, and re-layouts  69.1 us (14%)
  other arithmetic  17.2 us (4%)
  matrix products  15.1 us (3%)
  between operations  14.4 us (3%)
    all_to_all x1, waiting for transfers between devices, body(): lax.all_to_all(send_normed, 'expert', split_axis=1, concat_axis=1, tiled=...  69.3 us
    all_to_all x1, waiting for transfers between devices, body(): lax.all_to_all(grad_rows.reshape(slot_shape), 'expert', split_axis=1, con...  66.2 us
    all_to_all x1, waiting for transfers between devices, body(): lax.all_to_all(result.reshape(slot_shape), 'expert', split_axis=1, concat...  63.4 us
    all_to_all x1, waiting for transfers between devices, body(): lax.all_to_all(send_grad, 'expert', split_axis=1, concat_axis=1, tiled=True)  49.3 us
    all_to_all x1, starting transfers between devices, body(): lax.all_to_all(send_normed, 'expert', split_axis=1, concat_axis=1, tiled=...  39.4 us
    all_to_all x2, waiting for transfers between devices, copy_for_each(): lax.all_to_all(jnp.broadcast_to(value[None], (length, *value.shape)), axi...  30.3 us
    all_to_all x2, starting transfers between devices, copy_for_each(): lax.all_to_all(jnp.broadcast_to(value[None], (length, *value.shape)), axi...  19.2 us
  transfers between devices with their start and end apart: 7, of which 6 were waited for; matrix products, arithmetic and copies ran while one was open for 14% of the time, Pallas kernels for 0%

commit v1 on v0

v1 whole, which is shorter than its diff:
```python
import numpy as np
import jax
import jax.numpy as jnp
from jax import lax
from jax.experimental import pallas as pl
from jax.experimental.pallas import tpu as pltpu
from jax.sharding import Mesh, PartitionSpec as P

epsilon = 1e-06
BF = jnp.bfloat16
F32 = jnp.float32
I32 = jnp.int32
VMEM = pltpu.VMEM
LIMIT = 56 * 1024 * 1024

X, C, H, B, A, Y = 4, 2, 2, 2, 4, 4
PEERS = X * C * Y
TOK, D, FW, CAP = 128, 2048, 384, 6
PER = 4 * CAP
ROWS = PEERS * PER
GROUPS = 4
GROUP = ROWS // GROUPS
KIND = GROUP // 4
SLOTS = GROUPS * KIND


def sort_matrix():
    natural = np.arange(GROUP)
    place = (natural % PER) // CAP * KIND + natural // PER * CAP + natural % CAP
    to_natural = np.zeros((GROUP, GROUP), np.float32)
    to_natural[natural, place] = 1.0
    return to_natural


def whole(n):
    return [pl.BlockSpec(memory_space=VMEM)] * n


def params(**more):
    return pltpu.CompilerParams(vmem_limit_bytes=LIMIT, **more)


def split_kernel(gate_ref, up_ref, down_ref, out_ref):
    for e in range(2):
        for q in range(A):
            for m, ref in enumerate((gate_ref, up_ref)):
                for f in range(3):
                    out_ref[q, e, m, f * 32 : (f + 1) * 32, :] = ref[
                        e, q * 32 : (q + 1) * 32, f * 128 : (f + 1) * 128
                    ]
            out_ref[q, e, 2] = down_ref[e, q * 96 : (q + 1) * 96, :]


def split_weights(w_gate, w_up, w_down):
    return pl.pallas_call(
        split_kernel,
        out_shape=jax.ShapeDtypeStruct((A, 2, 3, 96, 128), BF),
        in_specs=whole(3),
        out_specs=pl.BlockSpec(memory_space=VMEM),
        compiler_params=params(),
        name="split_weights",
    )(w_gate, w_up, w_down)


def route_rows(ids0, ids1):
    labels = lax.broadcasted_iota(I32, (64, TOK), 0)
    m0, m1 = labels == ids0, labels == ids1
    one, zero = jnp.ones((64, TOK), F32), jnp.zeros((64, TOK), F32)
    both = (jnp.where(m0, one, zero) + jnp.where(m1, one, zero)).astype(BF)
    earlier = jnp.where(
        lax.broadcasted_iota(I32, (TOK, TOK), 0) < lax.broadcasted_iota(I32, (TOK, TOK), 1),
        jnp.ones((TOK, TOK), F32),
        jnp.zeros((TOK, TOK), F32),
    ).astype(BF)
    before = jnp.dot(both, earlier, preferred_element_type=F32)

    def row(ids, mask):
        position = jnp.sum(jnp.where(mask, before, zero), axis=0, keepdims=True).astype(I32)
        x, b = (ids >> 3) & 3, ids >> 5
        y, c = (ids >> 1) & 3, ids & 1
        return ((x * C + c) * Y + y) * PER + b * CAP + position

    return row(ids0, m0), row(ids1, m1)


def row_scale_of(hidden):
    return lax.rsqrt(jnp.mean(hidden * hidden, axis=1, keepdims=True) + epsilon)


def dispatch_kernel(ids_ref, hidden_ref, gain_ref, grad_ref, out_ref):
    hidden = hidden_ref[...].astype(F32)
    normed = (hidden * row_scale_of(hidden) * gain_ref[...]).astype(BF)
    both = jnp.concatenate([normed, grad_ref[...]], axis=0)
    r0, r1 = route_rows(ids_ref[0:1, :], ids_ref[1:2, :])
    one, zero = jnp.ones((GROUP, TOK), F32), jnp.zeros((GROUP, TOK), F32)
    for g in range(GROUPS):
        at = lax.broadcasted_iota(I32, (GROUP, TOK), 0) + g * GROUP
        picks = []
        for shift in (0, 2 * CAP):
            hit = (at == r0 + shift) | (at == r1 + shift)
            picks.append(jnp.where(hit, one, zero).astype(BF))
        chosen = jnp.concatenate(picks, axis=1)
        out_ref[g * GROUP : (g + 1) * GROUP, :] = jnp.dot(
            chosen, both, preferred_element_type=F32
        ).astype(BF)


def dispatch(ids, hidden, gain, grad):
    return pl.pallas_call(
        dispatch_kernel,
        out_shape=jax.ShapeDtypeStruct((ROWS, D), BF),
        in_specs=whole(4),
        out_specs=pl.BlockSpec(memory_space=VMEM),
        compiler_params=params(),
        name="dispatch",
    )(ids, hidden, gain, grad)


def sort_kernel(to_sorted_ref, rows_ref, out_ref):
    for g in range(GROUPS):
        block = jnp.dot(
            to_sorted_ref[...],
            rows_ref[g * GROUP : (g + 1) * GROUP, :],
            preferred_element_type=F32,
        ).astype(BF)
        for k in range(4):
            out_ref[k, g * KIND : (g + 1) * KIND, :] = block[k * KIND : (k + 1) * KIND, :]


def sort_rows(to_sorted, rows):
    return pl.pallas_call(
        sort_kernel,
        out_shape=jax.ShapeDtypeStruct((4, SLOTS, D), BF),
        in_specs=whole(2),
        out_specs=pl.BlockSpec(memory_space=VMEM),
        compiler_params=params(),
        name="sort_rows",
    )(to_sorted, rows)


def expert_kernel(rows_ref, to_natural_ref, w_ref, out_ref, in_mats, down_mat, sems):
    copies = []
    for b in range(B):
        mine = []
        for h in range(H):
            for q in range(A):
                z = (h * B + b) * A + q
                for m in range(2):
                    for f in range(3):
                        mine.append(
                            pltpu.make_async_copy(
                                w_ref.at[z, :, m, pl.ds(f * 32, 32), :],
                                in_mats.at[b, m, :, h, q, :, pl.ds(f * 128, 128)],
                                sems.at[b],
                            )
                        )
                mine.append(
                    pltpu.make_async_copy(
                        w_ref.at[z, :, 2, :, :],
                        down_mat.at[b, :, h, pl.ds(q * 96, 96), :],
                        sems.at[b],
                    )
                )
        copies.append(mine)
    for mine in copies:
        for c in mine:
            c.start()
    inner, d_gate, d_up = [], [], []
    for b in range(B):
        for c in copies[b]:
            c.wait()
        rows = rows_ref[b]
        gate_pre = jnp.dot(rows, in_mats[b, 0].reshape(D, FW), preferred_element_type=F32)
        up_pre = jnp.dot(rows, in_mats[b, 1].reshape(D, FW), preferred_element_type=F32)
        back = jnp.zeros((SLOTS, FW), F32)
        for k in range(8):
            chunk = jnp.concatenate([down_mat[b, k, 0], down_mat[b, k, 1]], axis=1)
            back = back + lax.dot_general(
                rows_ref[2 + b, :, k * 256 : (k + 1) * 256],
                chunk,
                (((1,), (1,)), ((), ())),
                preferred_element_type=F32,
            )
        s = jax.nn.sigmoid(gate_pre)
        silu = gate_pre * s
        inner.append((silu * up_pre).astype(BF))
        d_gate.append((back * up_pre * s * (1.0 + gate_pre * (1.0 - s))).astype(BF))
        d_up.append((back * silu).astype(BF))
    for k in range(8):
        parts = []
        for b in range(B):
            chunk = jnp.concatenate([down_mat[b, k, 0], down_mat[b, k, 1]], axis=1)
            parts.append(jnp.dot(inner[b], chunk, preferred_element_type=F32).astype(BF))
        for b in range(B):
            total = lax.dot_general(
                d_gate[b],
                in_mats[b, 0, k].reshape(256, FW),
                (((1,), (1,)), ((), ())),
                preferred_element_type=F32,
            ) + lax.dot_general(
                d_up[b],
                in_mats[b, 1, k].reshape(256, FW),
                (((1,), (1,)), ((), ())),
                preferred_element_type=F32,
            )
            parts.append(total.astype(BF))
        for g in range(GROUPS):
            block = jnp.concatenate([p[g * KIND : (g + 1) * KIND] for p in parts], axis=0)
            out_ref[g * GROUP : (g + 1) * GROUP, k * 256 : (k + 1) * 256] = jnp.dot(
                to_natural_ref[...], block, preferred_element_type=F32
            ).astype(BF)


def experts(rows, to_natural, weights):
    return pl.pallas_call(
        expert_kernel,
        out_shape=jax.ShapeDtypeStruct((ROWS, D), BF),
        in_specs=whole(2) + [pl.BlockSpec(memory_space=pl.ANY)],
        out_specs=pl.BlockSpec(memory_space=VMEM),
        scratch_shapes=[
            VMEM((B, 2, 8, H, A, 32, FW), BF),
            VMEM((B, 8, H, FW, 128), BF),
            pltpu.SemaphoreType.DMA((B,)),
        ],
        compiler_params=params(),
        name="experts",
    )(rows, to_natural, weights)


def combine_kernel(ids_ref, codes_ref, ret_ref, hidden_ref, gain_ref, grad_ref, out_ref, gin_ref):
    r0, r1 = route_rows(ids_ref[0:1, :], ids_ref[1:2, :])
    codes = codes_ref[...].astype(F32)
    weights = codes / (codes[0:1, :] + codes[1:2, :])
    lines = jnp.concatenate(
        [r0.astype(F32), r1.astype(F32), weights, jnp.zeros((TOK - 4, TOK), F32)], axis=0
    )
    columns = jnp.transpose(lines)
    c0, c1 = columns[:, 0:1].astype(I32), columns[:, 1:2].astype(I32)
    w0, w1 = columns[:, 2:3], columns[:, 3:4]
    at = lax.broadcasted_iota(I32, (TOK, ROWS), 1)
    one, zero = jnp.ones((TOK, ROWS), F32), jnp.zeros((TOK, ROWS), F32)
    chosen = jnp.concatenate(
        [
            jnp.where(at == c + shift, one, zero).astype(BF)
            for shift in (0, 2 * CAP)
            for c in (c0, c1)
        ],
        axis=0,
    )
    picked = jnp.dot(chosen, ret_ref[...], preferred_element_type=F32)
    mixture = picked[0:TOK] * w0 + picked[TOK : 2 * TOK] * w1
    grad_normed = picked[2 * TOK : 3 * TOK] * w0 + picked[3 * TOK :] * w1
    hidden = hidden_ref[...].astype(F32)
    row_scale = row_scale_of(hidden)
    out_ref[...] = (hidden + mixture).astype(BF)
    scaled = gain_ref[...] * grad_normed
    inner_mean = jnp.mean(scaled * hidden, axis=1, keepdims=True)
    gin_ref[...] = (
        grad_ref[...].astype(F32)
        + row_scale * scaled
        - hidden * ((row_scale * row_scale * row_scale) * inner_mean)
    ).astype(BF)


def combine(ids, codes, returned, hidden, gain, grad):
    shape = jax.ShapeDtypeStruct((TOK, D), BF)
    return pl.pallas_call(
        combine_kernel,
        out_shape=(shape, shape),
        in_specs=whole(6),
        out_specs=tuple(whole(2)),
        compiler_params=params(),
        name="combine",
    )(ids, codes, returned, hidden, gain, grad)


def exchange(rows):
    blocks = rows.reshape(PEERS, PER, D)
    return lax.all_to_all(blocks, ("X", "C", "Y"), 0, 0, tiled=True).reshape(ROWS, D)


def body(hidden_in, norm_gain, w_gate, w_up, w_down, expert_ids, gate_codes, out_grad):
    gain = norm_gain.reshape(1, D)
    ids, codes = expert_ids.T, gate_codes.T
    to_natural = sort_matrix()
    pieces = split_weights(w_gate, w_up, w_down)
    pieces = lax.all_to_all(pieces, "A", 0, 0, tiled=True)
    pieces = pieces.reshape(X * C, 3, 96, 128)
    pieces = lax.all_to_all(pieces, ("X", "C"), 0, 0, tiled=True)
    weights = lax.all_gather(pieces, ("H", "B", "A"), axis=0, tiled=False)
    arrived = exchange(dispatch(ids, hidden_in, gain, out_grad))
    rows = sort_rows(jnp.asarray(to_natural.T, BF), arrived)
    results = experts(rows, jnp.asarray(to_natural, BF), weights)
    returned = exchange(results)
    return combine(ids, codes, returned, hidden_in, gain, out_grad)


def solution(mesh):
    fine = Mesh(mesh.devices.reshape(X, C, H, B, A, Y), ("X", "C", "H", "B", "A", "Y"))
    tokens = P(("X", "C", "H", "B", "A", "Y"), None)
    owner, feature = ("B", "A", "Y"), ("X", "C", "H")
    in_specs = (
        tokens,
        P(),
        P(owner, feature, None),
        P(owner, feature, None),
        P(owner, None, feature),
        tokens,
        tokens,
        tokens,
    )
    return jax.shard_map(
        body, mesh=fine, in_specs=in_specs, out_specs=(tokens, tokens), check_vma=False
    )
```

time: 480 us -> 237 us (0.49)
  waiting for transfers between devices: 279 us -> 63.5 us
  blocking collectives: 0 us -> 129 us
  starting transfers between devices: 83.1 us -> 0.04 us
  local copies, waits for them, and re-layouts: 69.1 us -> 0 us
  Pallas kernels: 0 us -> 29.6 us
  other arithmetic: 17.2 us -> 0 us
  matrix products: 15.1 us -> 0 us
    all_to_all x6 -> x0, waiting for transfers between devices: 279 us -> none  [the longest x1 69.3 us: body(): lax.all_to_all(send_normed, 'expert', split_axis=1, concat_axis=1, tiled=...]
    all_to_all x0 -> x4, blocking collectives: none -> 129 us  [the longest x2 91.3 us: exchange(): lax.all_to_all(blocks, ('X', 'C', 'Y'), 0, 0, tiled=True).reshape(ROWS, D)]
    all_to_all x6 -> x0, starting transfers between devices: 83.1 us -> none  [the longest x1 39.4 us: body(): lax.all_to_all(send_normed, 'expert', split_axis=1, concat_axis=1, tiled=...]
    all_gather x1, waiting for transfers between devices: 0.02 us -> 63.5 us  [body(): weights = lax.all_gather(pieces, ('H', 'B', 'A'), axis=0, tiled=False)]
    pallas_call x0 -> x5, Pallas kernels: none -> 29.6 us  [the longest x1 13.6 us: experts(): pl.pallas_call(expert_kernel, out_shape=jax.ShapeDtypeStruct((ROWS, D), B...]
    gather x6 -> x0, local copies, waits for them, and re-layouts: 16.2 us -> none  [the longest x2 6.8 us: body(): normed[order_rows]]
    dot_general x6 -> x0, matrix products: 15.1 us -> none  [the longest x1 3.82 us: expert_forward(): gate_pre = jnp.dot(slot_rows, gate_mat, preferred_element_type=jnp.float32)]
    reshape x6 -> x0, local copies, waits for them, and re-layouts: 14.8 us -> none  [the longest x2 9.33 us: gather_turned(): section = filled[:, at:at + t[0].size].reshape(-1, *t.shape[1:])]
  transfers between devices with their start and end apart: 7 -> 1, of which waited for: 6 -> 1; matrix products, arithmetic and copies ran while one was open for 14% -> 0% of each run, Pallas kernels for 0% -> 4%
where the time goes in v1:
time: 237 us; the launch traced here: 236 us
  blocking collectives  129 us (54%)
  waiting for transfers between devices  63.5 us (27%)
  Pallas kernels  29.6 us (12%)
  between operations  14 us (6%)
    all_to_all x2, blocking collectives, exchange(): lax.all_to_all(blocks, ('X', 'C', 'Y'), 0, 0, tiled=True).reshape(ROWS, D)  91.3 us
    all_gather x1, waiting for transfers between devices, body(): weights = lax.all_gather(pieces, ('H', 'B', 'A'), axis=0, tiled=False)  63.5 us
    all_to_all x1, blocking collectives, body(): pieces = lax.all_to_all(pieces, 'A', 0, 0, tiled=True)  20.9 us
    all_to_all x1, blocking collectives, body(): pieces = lax.all_to_all(pieces, ('X', 'C'), 0, 0, tiled=True)  16.9 us
    pallas_call x1, Pallas kernels, experts(): pl.pallas_call(expert_kernel, out_shape=jax.ShapeDtypeStruct((ROWS, D), B...  13.6 us
    pallas_call x1, Pallas kernels, combine(): pl.pallas_call(combine_kernel, out_shape=(shape, shape), in_specs=whole(6...  5.32 us
  transfers between devices with their start and end apart: 1, of which 1 were waited for; matrix products, arithmetic and copies ran while one was open for 0% of the time, Pallas kernels for 4%

profile of v1, /device:TPU:1, one launch (start us, length us, event | category | flops | bytes accessed | tf_op | source)
XLA Modules:
  0.0 236.2 jit_solution(16030712422502293150)
XLA Ops:
  7.2 0.0 all-gather.3.cloned.1.call-start
  7.2 2.0 split_weights.1
  9.2 20.9 %all_to_all.20 = bf16[4,2,3,96,128]{4,3,2,1,0:T(8,128)(2,1)S(1)} all-to-all(bf16[4,2,3,96,128]{4,3,2,1,0:T(8,128)(2,1)} %split_weights.1), channel_id=1, replica_groups=mesh['X'=4,'C'=2,'H'=2,'B'=2,'A'=4,'Y'=4] {'A'}, dimensions={0} | all-to-all | bytes 1179648 | tf_op jit(solution)/shard_map/all_to_all | solution.py:287
  30.1 16.9 %all_to_all.21 = bf16[8,3,96,128]{3,2,1,0:T(8,128)(2,1)} all-to-all(bf16[8,3,96,128]{3,2,1,0:T(8,128)(2,1)S(1)} %bitcast.14), channel_id=1, replica_groups=mesh['X'=4,'C'=2,'H'=2,'B'=2,'A'=4,'Y'=4] {'X','C'}, dimensions={0} | all-to-all | bytes 1179648 | tf_op jit(solution)/shard_map/all_to_all | solution.py:289
  47.0 0.0 all-gather.3.cloned.1.call-update
  47.0 4.1 %dispatch.1 = bf16[768,2048]{1,0:T(8,128)(2,1)} custom-call(s32[2,128]{1,0:T(2,128)} %bitcast.17, bf16[128,2048]{1,0:T(8,128)(2,1)} %hidden_ref.3, f32[1,2048]{1,0:T(1,128)} %bitcast.15, bf16[128,2048]{1,0:T(8,128)(2,1)} %grad_ref.3), custom_call_target="tpu_custom_call" | custom-call | tf_op jit(solution)/shard_map/dispatch/pallas_call | solution.py:109
  51.1 44.8 %all_to_all.22 = bf16[32,24,2048]{2,1,0:T(8,128)(2,1)} all-to-all(bf16[32,24,2048]{2,1,0:T(8,128)(2,1)} %bitcast.10), channel_id=1, replica_groups=mesh['X'=4,'C'=2,'H'=2,'B'=2,'A'=4,'Y'=4] {'X','C','Y'}, dimensions={0} | all-to-all | bytes 6291456 | tf_op jit(solution)/shard_map/all_to_all | solution.py:279
  95.9 4.6 %sort_rows.1.rows_ref = bf16[4,192,2048]{2,1,0:T(8,128)(2,1)} custom-call(bf16[192,192]{1,0:T(8,128)(2,1)} %constant.4.clone.to_sorted_ref, bf16[768,2048]{1,0:T(8,128)(2,1)} %bitcast.9), custom_call_target="tpu_custom_call" | custom-call | tf_op jit(solution)/shard_map/sort_rows/pallas_call | solution.py:131
  100.5 63.5 %all-gather.3.cloned.1.call-done = bf16[128,3,96,128]{3,2,1,0:T(8,128)(2,1)} async-done(((bf16[8,3,96,128]{3,2,1,0:T(8,128)(2,1)}), bf16[128,3,96,128]{3,2,1,0:T(8,128)(2,1)}) %all-gather.3.cloned.1.call-update) | async-done | bytes 9437200 | tf_op jit(solution)/shard_map/all_gather | solution.py:290
  163.9 13.6 %experts.1 = bf16[768,2048]{1,0:T(8,128)(2,1)} custom-call(bf16[4,192,2048]{2,1,0:T(8,128)(2,1)} %sort_rows.1.rows_ref, bf16[192,192]{1,0:T(8,128)(2,1)} %constant.5.clone.to_natural_ref, bf16[16,8,3,96,128]{4,3,2,1,0:T(8,128)(2,1)} %bitcast.13), custom_call_target="tpu_custom_call" | custom-call | tf_op jit(solution)/shard_map/experts/pallas_call | solution.py:215
  177.6 46.5 %all_to_all.23 = bf16[32,24,2048]{2,1,0:T(8,128)(2,1)} all-to-all(bf16[32,24,2048]{2,1,0:T(8,128)(2,1)} %bitcast.12), channel_id=1, replica_groups=mesh['X'=4,'C'=2,'H'=2,'B'=2,'A'=4,'Y'=4] {'X','C','Y'}, dimensions={0} | all-to-all | bytes 6291456 | tf_op jit(solution)/shard_map/all_to_all | solution.py:279
  224.1 5.3 %combine.1 = (bf16[128,2048]{1,0:T(8,128)(2,1)}, bf16[128,2048]{1,0:T(8,128)(2,1)}) custom-call(s32[2,128]{1,0:T(2,128)} %bitcast.18, s32[2,128]{1,0:T(2,128)} %bitcast.19, bf16[768,2048]{1,0:T(8,128)(2,1)} %bitcast.11, bf16[128,2048]{1,0:T(8,128)(2,1)} %hidden_ref.3, f32[1,2048]{1,0:T(1,128)} %bitcast.16, bf16[128,2048]{1,0:T(8,128)(2,1)} %grad_ref.3), custom_call_target="tpu_custom_call" | custom-call | tf_op jit(solution)/shard_map/combine/pallas_call | solution.py:267
Async XLA Ops:
  7.2 156.8 %all-gather.3.cloned.1.call-start = ((), (), s32[]{:S(2)}) async-start(), calls=%async_computation.4 | async-start | bytes 10027008 | tf_op jit(solution)/shard_map/all_gather | solution.py:290
Sparse Core Ops, SparseCore 0:
  47.1 116.7 all-gather.2

commit v2 on v1

--- a/solution.py
+++ b/solution.py
@@ -11,7 +11,7 @@
 F32 = jnp.float32
 I32 = jnp.int32
 VMEM = pltpu.VMEM
-LIMIT = 56 * 1024 * 1024
+MIB = 1024 * 1024
 
 X, C, H, B, A, Y = 4, 2, 2, 2, 4, 4
 PEERS = X * C * Y
@@ -36,30 +36,64 @@
     return [pl.BlockSpec(memory_space=VMEM)] * n
 
 
-def params(**more):
-    return pltpu.CompilerParams(vmem_limit_bytes=LIMIT, **more)
-
-
-def split_kernel(gate_ref, up_ref, down_ref, out_ref):
-    for e in range(2):
-        for q in range(A):
+def params(mib=24):
+    return pltpu.CompilerParams(vmem_limit_bytes=mib * MIB)
+
+
+def split_kernel(gate_ref, up_ref, down_ref, *out_refs):
+    x = lax.axis_index("X")
+    for r in range(X):
+        q = (x + r) & 3
+        for e in range(2):
             for m, ref in enumerate((gate_ref, up_ref)):
                 for f in range(3):
-                    out_ref[q, e, m, f * 32 : (f + 1) * 32, :] = ref[
-                        e, q * 32 : (q + 1) * 32, f * 128 : (f + 1) * 128
+                    out_refs[r][e, m, f * 32 : (f + 1) * 32, :] = ref[
+                        e, pl.ds(pl.multiple_of(q * 32, 32), 32), f * 128 : (f + 1) * 128
                     ]
-            out_ref[q, e, 2] = down_ref[e, q * 96 : (q + 1) * 96, :]
+            out_refs[r][e, 2] = down_ref[e, pl.ds(pl.multiple_of(q * 96, 32), 96), :]
 
 
 def split_weights(w_gate, w_up, w_down):
     return pl.pallas_call(
         split_kernel,
-        out_shape=jax.ShapeDtypeStruct((A, 2, 3, 96, 128), BF),
+        out_shape=(jax.ShapeDtypeStruct((2, 3, 96, 128), BF),) * X,
         in_specs=whole(3),
-        out_specs=pl.BlockSpec(memory_space=VMEM),
+        out_specs=tuple(whole(X)),
         compiler_params=params(),
         name="split_weights",
     )(w_gate, w_up, w_down)
+
+
+def send_home(pieces):
+    moved = []
+    for r in range(X):
+        pairs = [(x * A + a, a * A + (x + r) % X) for x in range(X) for a in range(A)]
+        moved.append(lax.ppermute(pieces[r], ("X", "A"), pairs))
+    return moved
+
+
+def place_kernel(*refs):
+    out_ref, sem = refs[X:]
+    a = lax.axis_index("A")
+    copies = [
+        pltpu.make_async_copy(refs[r], out_ref.at[:, (a - r) & 3], sem) for r in range(X)
+    ]
+    for copy in copies:
+        copy.start()
+    for copy in copies:
+        copy.wait()
+
+
+def place(pieces):
+    return pl.pallas_call(
+        place_kernel,
+        out_shape=pltpu.VMEM((2, X, 3, 96, 128), BF),
+        in_specs=[pl.BlockSpec(memory_space=pl.ANY)] * X,
+        out_specs=pl.BlockSpec(memory_space=VMEM),
+        scratch_shapes=[pltpu.SemaphoreType.DMA],
+        compiler_params=params(),
+        name="place",
+    )(*pieces)
 
 
 def route_rows(ids0, ids1):
@@ -108,12 +142,17 @@
 def dispatch(ids, hidden, gain, grad):
     return pl.pallas_call(
         dispatch_kernel,
-        out_shape=jax.ShapeDtypeStruct((ROWS, D), BF),
+        out_shape=pltpu.VMEM((ROWS, D), BF),
         in_specs=whole(4),
         out_specs=pl.BlockSpec(memory_space=VMEM),
         compiler_params=params(),
         name="dispatch",
     )(ids, hidden, gain, grad)
+
+
+def lanes(n):
+    c, x = n // X, n % X
+    return (x * C + c) * 256
 
 
 def sort_kernel(to_sorted_ref, rows_ref, out_ref):
@@ -124,13 +163,17 @@
             preferred_element_type=F32,
         ).astype(BF)
         for k in range(4):
-            out_ref[k, g * KIND : (g + 1) * KIND, :] = block[k * KIND : (k + 1) * KIND, :]
+            for n in range(8):
+                at = lanes(n)
+                out_ref[k, g * KIND : (g + 1) * KIND, n * 256 : (n + 1) * 256] = block[
+                    k * KIND : (k + 1) * KIND, at : at + 256
+                ]
 
 
 def sort_rows(to_sorted, rows):
     return pl.pallas_call(
         sort_kernel,
-        out_shape=jax.ShapeDtypeStruct((4, SLOTS, D), BF),
+        out_shape=pltpu.VMEM((4, SLOTS, D), BF),
         in_specs=whole(2),
         out_specs=pl.BlockSpec(memory_space=VMEM),
         compiler_params=params(),
@@ -206,7 +249,7 @@
             parts.append(total.astype(BF))
         for g in range(GROUPS):
             block = jnp.concatenate([p[g * KIND : (g + 1) * KIND] for p in parts], axis=0)
-            out_ref[g * GROUP : (g + 1) * GROUP, k * 256 : (k + 1) * 256] = jnp.dot(
+            out_ref[g * GROUP : (g + 1) * GROUP, lanes(k) : lanes(k) + 256] = jnp.dot(
                 to_natural_ref[...], block, preferred_element_type=F32
             ).astype(BF)
 
@@ -214,15 +257,15 @@
 def experts(rows, to_natural, weights):
     return pl.pallas_call(
         expert_kernel,
-        out_shape=jax.ShapeDtypeStruct((ROWS, D), BF),
-        in_specs=whole(2) + [pl.BlockSpec(memory_space=pl.ANY)],
+        out_shape=pltpu.VMEM((ROWS, D), BF),
+        in_specs=whole(2) + [pl.BlockSpec(memory_space=pltpu.HBM)],
         out_specs=pl.BlockSpec(memory_space=VMEM),
         scratch_shapes=[
             VMEM((B, 2, 8, H, A, 32, FW), BF),
             VMEM((B, 8, H, FW, 128), BF),
             pltpu.SemaphoreType.DMA((B,)),
         ],
-        compiler_params=params(),
+        compiler_params=params(54),
         name="experts",
     )(rows, to_natural, weights)
 
@@ -283,13 +326,12 @@
     gain = norm_gain.reshape(1, D)
     ids, codes = expert_ids.T, gate_codes.T
     to_natural = sort_matrix()
-    pieces = split_weights(w_gate, w_up, w_down)
-    pieces = lax.all_to_all(pieces, "A", 0, 0, tiled=True)
-    pieces = pieces.reshape(X * C, 3, 96, 128)
-    pieces = lax.all_to_all(pieces, ("X", "C"), 0, 0, tiled=True)
+    pieces = place(send_home(split_weights(w_gate, w_up, w_down)))
+    pieces = lax.all_to_all(pieces, "C", 0, 0, tiled=True).reshape(C * X, 3, 96, 128)
     weights = lax.all_gather(pieces, ("H", "B", "A"), axis=0, tiled=False)
     arrived = exchange(dispatch(ids, hidden_in, gain, out_grad))
     rows = sort_rows(jnp.asarray(to_natural.T, BF), arrived)
+    rows = pltpu.with_memory_space_constraint(rows, VMEM)
     results = experts(rows, jnp.asarray(to_natural, BF), weights)
     returned = exchange(results)
     return combine(ids, codes, returned, hidden_in, gain, out_grad)

time: 237 us -> 230 us (0.970)
  blocking collectives: 129 us -> 97.4 us
  starting transfers between devices: 0.04 us -> 18.2 us
  waiting for transfers between devices: 63.5 us -> 79.5 us
  Pallas kernels: 29.6 us -> 16.8 us
  local copies, waits for them, and re-layouts: 0 us -> 2.89 us
    all_to_all x2 -> x1, blocking collectives: 37.8 us -> 5.08 us  [body(): lax.all_to_all(pieces, 'C', 0, 0, tiled=True).reshape(C * X, 3, 96, 128)]
    ppermute x0 -> x4, starting transfers between devices: none -> 18.2 us  [send_home(): moved.append(lax.ppermute(pieces[r], ('X', 'A'), pairs))]
    pallas_call x4 -> x5, Pallas kernels: 24.3 us -> 13.6 us  [the longest x1 11 us: experts(): pl.pallas_call(expert_kernel, out_shape=pltpu.VMEM((ROWS, D), BF), in_spe...]
    ppermute x0 -> x4, waiting for transfers between devices: none -> 8.1 us  [send_home(): moved.append(lax.ppermute(pieces[r], ('X', 'A'), pairs))]
    all_gather x1, waiting for transfers between devices: 63.5 us -> 71.4 us  [body(): weights = lax.all_gather(pieces, ('H', 'B', 'A'), axis=0, tiled=False)]
    unnamed x0 -> x22, local copies, waits for them, and re-layouts: none -> 2.89 us
  transfers between devices with their start and end apart: 1 -> 5, of which waited for: 1 -> 2; matrix products, arithmetic and copies ran while one was open for 0% -> 0% of each run, Pallas kernels for 4% -> 1%
where the time goes in v2:
time: 230 us; the launch traced here: 229 us
  blocking collectives  97.4 us (42%)
  waiting for transfers between devices  79.5 us (35%)
  starting transfers between devices  18.2 us (8%)
  Pallas kernels  16.8 us (7%)
  between operations  14.2 us (6%)
  local copies, waits for them, and re-layouts  2.89 us (1%)
    all_to_all x2, blocking collectives, exchange(): lax.all_to_all(blocks, ('X', 'C', 'Y'), 0, 0, tiled=True).reshape(ROWS, D)  92.3 us
    all_gather x1, waiting for transfers between devices, body(): weights = lax.all_gather(pieces, ('H', 'B', 'A'), axis=0, tiled=False)  71.4 us
    ppermute x4, starting transfers between devices, send_home(): moved.append(lax.ppermute(pieces[r], ('X', 'A'), pairs))  18.2 us
    pallas_call x1, Pallas kernels, experts(): pl.pallas_call(expert_kernel, out_shape=pltpu.VMEM((ROWS, D), BF), in_spe...  11 us
    ppermute x4, waiting for transfers between devices, send_home(): moved.append(lax.ppermute(pieces[r], ('X', 'A'), pairs))  8.1 us
    all_to_all x1, blocking collectives, body(): lax.all_to_all(pieces, 'C', 0, 0, tiled=True).reshape(C * X, 3, 96, 128)  5.08 us
  transfers between devices with their start and end apart: 5, of which 2 were waited for; matrix products, arithmetic and copies ran while one was open for 0% of the time, Pallas kernels for 1%

profile of v2, /device:TPU:1, one launch (start us, length us, event | category | flops | bytes accessed | tf_op | source)
XLA Modules:
  0.0 229.1 jit_solution(13719541463005312936)
XLA Ops:
  7.2 0.0 copy-start
  7.2 0.0 all-gather.2.cloned.1.call-start
  7.2 1.0 copy-done.4
  8.2 0.9 copy-done.5
  9.2 0.9 copy-done.6
  10.1 0.1 split_weights.1
  10.2 0.7 collective-permute-start
  10.9 6.4 %collective-permute-start.1 = (bf16[2,3,96,128]{3,2,1,0:T(8,128)(2,1)S(1)}, bf16[2,3,96,128]{3,2,1,0:T(8,128)(2,1)S(1)}, u32[]{:S(2)}, u32[]{:S(2)}) collective-permute-start(bf16[2,3,96,128]{3,2,1,0:T(8,128)(2,1)S(1)} %get-tuple-element.7), channel_id=1, source_target_pairs={{0,4},{4,132},{8,260},{12,388},{128,8},{132,136},{136,264},{140,39... | collective-permute-start | bytes 442376 | tf_op jit(solution)/shard_map/ppermute | solution.py:71
  17.2 6.4 %collective-permute-start.2 = (bf16[2,3,96,128]{3,2,1,0:T(8,128)(2,1)S(1)}, bf16[2,3,96,128]{3,2,1,0:T(8,128)(2,1)S(1)}, u32[]{:S(2)}, u32[]{:S(2)}) collective-permute-start(bf16[2,3,96,128]{3,2,1,0:T(8,128)(2,1)S(1)} %get-tuple-element.8), channel_id=1, source_target_pairs={{0,8},{4,136},{8,264},{12,392},{128,12},{132,140},{136,268},{140,3... | collective-permute-start | bytes 442376 | tf_op jit(solution)/shard_map/ppermute | solution.py:71
  23.6 4.8 %collective-permute-start.3 = (bf16[2,3,96,128]{3,2,1,0:T(8,128)(2,1)S(1)}, bf16[2,3,96,128]{3,2,1,0:T(8,128)(2,1)S(1)}, u32[]{:S(2)}, u32[]{:S(2)}) collective-permute-start(bf16[2,3,96,128]{3,2,1,0:T(8,128)(2,1)S(1)} %get-tuple-element.9), channel_id=1, source_target_pairs={{0,12},{4,140},{8,268},{12,396},{128,0},{132,128},{136,256},{140,3... | collective-permute-start | bytes 442376 | tf_op jit(solution)/shard_map/ppermute | solution.py:71
  28.5 8.1 %collective-permute-done.3.refs_3_ = bf16[2,3,96,128]{3,2,1,0:T(8,128)(2,1)S(1)} collective-permute-done((bf16[2,3,96,128]{3,2,1,0:T(8,128)(2,1)S(1)}, bf16[2,3,96,128]{3,2,1,0:T(8,128)(2,1)S(1)}, u32[]{:S(2)}, u32[]{:S(2)}) %collective-permute-start.3) | collective-permute-done | bytes 147488 | tf_op jit(solution)/shard_map/ppermute | solution.py:71
  36.5 0.4 place.1
  36.9 5.1 %all_to_all.15 = bf16[2,4,3,96,128]{4,3,2,1,0:T(8,128)(2,1)} all-to-all(bf16[2,4,3,96,128]{4,3,2,1,0:T(8,128)(2,1)S(1)} %place.1), channel_id=1, replica_groups=mesh['X'=4,'C'=2,'H'=2,'B'=2,'A'=4,'Y'=4] {'C'}, dimensions={0} | all-to-all | bytes 1179648 | tf_op jit(solution)/shard_map/all_to_all | solution.py:330
  42.0 0.0 all-gather.2.cloned.1.call-update
  42.1 1.2 dispatch.1
  43.3 0.0 copy-start.7
  43.3 46.0 %all_to_all.16 = bf16[32,24,2048]{2,1,0:T(8,128)(2,1)S(1)} all-to-all(bf16[32,24,2048]{2,1,0:T(8,128)(2,1)S(1)} %bitcast.9), channel_id=1, replica_groups=mesh['X'=4,'C'=2,'H'=2,'B'=2,'A'=4,'Y'=4] {'X','C','Y'}, dimensions={0} | all-to-all | bytes 6291456 | tf_op jit(solution)/shard_map/all_to_all | solution.py:322
  89.3 1.0 sort_rows.1.rows_ref
  90.3 71.4 %all-gather.2.cloned.1.call-done.w_ref = bf16[16,8,3,96,128]{4,3,2,1,0:T(8,128)(2,1)} async-done(((bf16[1,8,3,96,128]{4,3,2,1,0:T(8,128)(2,1)}), bf16[16,8,3,96,128]{4,3,2,1,0:T(8,128)(2,1)}) %all-gather.2.cloned.1.call-update) | async-done | bytes 9437200 | tf_op jit(solution)/shard_map/all_gather | solution.py:331
  161.7 11.0 %experts.1 = bf16[768,2048]{1,0:T(8,128)(2,1)S(1)} custom-call(bf16[4,192,2048]{2,1,0:T(8,128)(2,1)S(1)} %sort_rows.1.rows_ref, bf16[192,192]{1,0:T(8,128)(2,1)} %constant.5.clone.to_natural_ref, bf16[16,8,3,96,128]{4,3,2,1,0:T(8,128)(2,1)} %all-gather.2.cloned.1.call-done.w_ref), custom_call_target="tpu_custom_call" | custom-call | tf_op jit(solution)/shard_map/experts/pallas_call | solution.py:258
  172.7 0.0 copy-start.3
  172.7 0.0 copy-start.10
  172.7 46.3 %all_to_all.17 = bf16[32,24,2048]{2,1,0:T(8,128)(2,1)S(1)} all-to-all(bf16[32,24,2048]{2,1,0:T(8,128)(2,1)S(1)} %bitcast.11), channel_id=1, replica_groups=mesh['X'=4,'C'=2,'H'=2,'B'=2,'A'=4,'Y'=4] {'X','C','Y'}, dimensions={0} | all-to-all | bytes 6291456 | tf_op jit(solution)/shard_map/all_to_all | solution.py:322
  219.1 3.2 %combine.1 = (bf16[128,2048]{1,0:T(8,128)(2,1)}, bf16[128,2048]{1,0:T(8,128)(2,1)}) custom-call(s32[2,128]{1,0:T(2,128)S(1)} %bitcast.15, s32[2,128]{1,0:T(2,128)S(1)} %bitcast.16, bf16[768,2048]{1,0:T(8,128)(2,1)S(1)} %bitcast.10, bf16[128,2048]{1,0:T(8,128)(2,1)S(1)} %copy-done.1, f32[1,2048]{1,0:T(1,128)S(1)} %bitcast.13, bf16[128,2048]{1,0:T(8,128)(2,1)S(1)} %copy-done.3), custom_call_target="tpu_custom_call" | custom-call | tf_op jit(solution)/shard_map/combine/pallas_call | solution.py:310
  (18 shorter events, 0.0 us)
Async XLA Ops:
  7.2 34.9 %copy-start = (bf16[128,2048]{1,0:T(8,128)(2,1)S(1)}, bf16[128,2048]{1,0:T(8,128)(2,1)}, u32[]{:S(2)}) copy-start(bf16[128,2048]{1,0:T(8,128)(2,1)} %hidden_ref.3) | copy-start | bytes 1572868
  7.2 34.8 %copy-start.2 = (bf16[128,2048]{1,0:T(8,128)(2,1)S(1)}, bf16[128,2048]{1,0:T(8,128)(2,1)}, u32[]{:S(2)}) copy-start(bf16[128,2048]{1,0:T(8,128)(2,1)} %grad_ref.3) | copy-start | bytes 1572868
  7.2 154.5 %all-gather.2.cloned.1.call-start = ((), (), s32[]{:S(2)}) async-start(), calls=%async_computation.3 | async-start | bytes 10027008 | tf_op jit(solution)/shard_map/all_gather | solution.py:331
  7.2 1.0 copy-start.4
  8.2 0.9 copy-start.5
  9.2 0.9 copy-start.6
  10.1 31.9 %copy-start.8 = (f32[2048]{0:T(1024)S(1)}, f32[2048]{0:T(1024)}, u32[]{:S(2)}) copy-start(f32[2048]{0:T(1024)} %param.11) | copy-start | bytes 24580
  10.1 32.0 %copy-start.9 = (s32[128,2]{0,1:T(2,128)S(1)}, s32[128,2]{0,1:T(2,128)}, u32[]{:S(2)}) copy-start(s32[128,2]{0,1:T(2,128)} %param.15) | copy-start | bytes 3076
  10.2 18.2 %collective-permute-start = (bf16[2,3,96,128]{3,2,1,0:T(8,128)(2,1)S(1)}, bf16[2,3,96,128]{3,2,1,0:T(8,128)(2,1)S(1)}, u32[]{:S(2)}, u32[]{:S(2)}) collective-permute-start(bf16[2,3,96,128]{3,2,1,0:T(8,128)(2,1)S(1)} %get-tuple-element.6), channel_id=1, source_target_pairs={{0,0},{4,128},{8,256},{12,384},{128,4},{132,132},{136,260},{140,38... | collective-permute-start | bytes 442376 | tf_op jit(solution)/shard_map/ppermute | solution.py:71
  10.9 17.6 %collective-permute-start.1 = (bf16[2,3,96,128]{3,2,1,0:T(8,128)(2,1)S(1)}, bf16[2,3,96,128]{3,2,1,0:T(8,128)(2,1)S(1)}, u32[]{:S(2)}, u32[]{:S(2)}) collective-permute-start(bf16[2,3,96,128]{3,2,1,0:T(8,128)(2,1)S(1)} %get-tuple-element.7), channel_id=1, source_target_pairs={{0,4},{4,132},{8,260},{12,388},{128,8},{132,136},{136,264},{140,39... | collective-permute-start | bytes 442376 | tf_op jit(solution)/shard_map/ppermute | solution.py:71
  17.2 11.2 %collective-permute-start.2 = (bf16[2,3,96,128]{3,2,1,0:T(8,128)(2,1)S(1)}, bf16[2,3,96,128]{3,2,1,0:T(8,128)(2,1)S(1)}, u32[]{:S(2)}, u32[]{:S(2)}) collective-permute-start(bf16[2,3,96,128]{3,2,1,0:T(8,128)(2,1)S(1)} %get-tuple-element.8), channel_id=1, source_target_pairs={{0,8},{4,136},{8,264},{12,392},{128,12},{132,140},{136,268},{140,3... | collective-permute-start | bytes 442376 | tf_op jit(solution)/shard_map/ppermute | solution.py:71
  23.6 12.9 %collective-permute-start.3 = (bf16[2,3,96,128]{3,2,1,0:T(8,128)(2,1)S(1)}, bf16[2,3,96,128]{3,2,1,0:T(8,128)(2,1)S(1)}, u32[]{:S(2)}, u32[]{:S(2)}) collective-permute-start(bf16[2,3,96,128]{3,2,1,0:T(8,128)(2,1)S(1)} %get-tuple-element.9), channel_id=1, source_target_pairs={{0,12},{4,140},{8,268},{12,396},{128,0},{132,128},{136,256},{140,3... | collective-permute-start | bytes 442376 | tf_op jit(solution)/shard_map/ppermute | solution.py:71
  43.3 46.0 %copy-start.7 = (bf16[192,192]{1,0:T(8,128)(2,1)S(1)}, bf16[192,192]{1,0:T(8,128)(2,1)}, u32[]{:S(2)}) copy-start(bf16[192,192]{1,0:T(8,128)(2,1)} %constant.4.clone.to_sorted_ref) | copy-start | bytes 221188
  172.7 46.4 %copy-start.1 = (bf16[128,2048]{1,0:T(8,128)(2,1)S(1)}, bf16[128,2048]{1,0:T(8,128)(2,1)}, u32[]{:S(2)}) copy-start(bf16[128,2048]{1,0:T(8,128)(2,1)} %hidden_ref.3) | copy-start | bytes 1572868
  172.7 46.4 %copy-start.3 = (bf16[128,2048]{1,0:T(8,128)(2,1)S(1)}, bf16[128,2048]{1,0:T(8,128)(2,1)}, u32[]{:S(2)}) copy-start(bf16[128,2048]{1,0:T(8,128)(2,1)} %grad_ref.3) | copy-start | bytes 1572868
  172.7 46.4 %copy-start.10 = (s32[128,2]{0,1:T(2,128)S(1)}, s32[128,2]{0,1:T(2,128)}, u32[]{:S(2)}) copy-start(s32[128,2]{0,1:T(2,128)} %param.16) | copy-start | bytes 3076
Sparse Core Ops, SparseCore 0:
  42.1 119.4 all-gather.1
